TPU v7x, 128 devices: a whole 4x4x4 slice. The times are simulated.
128 devices in a mesh: sx: 8 (over y, core), sy: 16 (over x, z).
Axes of the slice: x: 4, y: 4, z: 4, core: 2. Of those that a mesh axis runs over, the one named last changes fastest.
Arguments:
- loads: float32 [8, 16, 1536, 256], P('sx', 'sy')
- schur_flex: float32 [8, 16, 1536, 1536], P('sx', 'sy'), as said below
- dirichlet: float32 [8, 16, 1536, 1536], P('sx', 'sy'), as said below
- coupling: float32 [8, 16, 16, 1536], P('sx', 'sy'), may hold values from -0.3125 to 0.3125
- corner_index: int32 [8, 16, 16], P('sx', 'sy'), may hold values from 0 to 512, as said below
- face_lists: int32 [8, 16, 4, 384], P('sx', 'sy'), may hold values from 0 to 383, as said below
- coarse_inverse: float32 [512, 512], P(('sx', 'sy')), as said below
Outputs:
- multipliers: float32 [8, 16, 1536, 256], P('sx', 'sy')
- residual: float32 [8, 16, 1536, 256], P('sx', 'sy')
Inputs may be any that keep to these rules, and one draw needn't show every extreme that they name: `corner_index`: each subdomain lists 4 coarse dofs for each of its four corners; 512 marks a corner on the clamped edges of the panel, which has no coarse dof; every coarse dof below 512 is named by some subdomain. `face_lists`: each face's list is a permutation of the 384 dofs of the facing face; the facing lists of two neighbouring subdomains are inverse permutations. `schur_flex`: symmetric positive definite for every subdomain. `dirichlet`: symmetric positive definite for every subdomain. `coarse_inverse`: symmetric positive definite.
All inputs are finite; a program needn't handle non-finite values.
Results may differ from a plain program's by a relative error of at most 0.00017.
Values sent between devices are 32-bit elements; how exact they have to be, the bound alone decides.
A program may use at most 128 MiB of HBM per device.

v0:
```python
import jax
import jax.numpy as jnp
from jax import lax
from jax.sharding import PartitionSpec as P

ITERS = 2


def shifted(block, axis, distance):
    devices = range(lax.axis_size(axis))
    route = [(i - distance, i) for i in devices if i - distance in devices]
    return lax.ppermute(block, axis, route)


def jump(field, face_index):
    size = field.shape[0] // 4
    width = field.shape[1]
    face_rows = field.reshape(4, size, width)
    from_low_x = shifted(face_rows[1], "sx", 1)
    from_high_x = shifted(face_rows[0], "sx", -1)
    from_low_y = shifted(face_rows[3], "sy", 1)
    from_high_y = shifted(face_rows[2], "sy", -1)
    received = jnp.stack([from_low_x, from_high_x, from_low_y, from_high_y], axis=0)
    matched = received[jnp.arange(4, dtype=jnp.int32)[:, None], face_index]
    return (face_rows - matched).reshape(4 * size, width)


def coarse_solve(coarse_rhs, stiffness_inverse_lines):
    highest = lax.Precision.HIGHEST
    total = lax.psum(coarse_rhs, ("sx", "sy"))
    mine = jnp.dot(stiffness_inverse_lines, total, precision=highest)
    return lax.all_gather(mine, ("sx", "sy"), axis=0, tiled=True)


def inner(first, second):
    return jnp.sum(first * second, axis=0)


def shards(loads, schur_flex, dirichlet, coupling, corner_index, face_lists, coarse_inverse):
    highest = lax.Precision.HIGHEST
    flex_mat = schur_flex[0, 0]
    prec_mat = dirichlet[0, 0]
    coupling_mat = coupling[0, 0]
    corners = corner_index[0, 0]
    face_index = face_lists[0, 0]
    ncoarse = coarse_inverse.shape[1]
    onehot = (corners[None, :] == jnp.arange(ncoarse, dtype=jnp.int32)[:, None]).astype(jnp.float32)

    def precondition(dual_vector):
        spread = jump(dual_vector, face_index)
        operator_applied = jnp.dot(prec_mat, spread, precision=highest)
        return 0.5 * jump(operator_applied, face_index)

    def residual_dot(residual, precond):
        return lax.psum(inner(residual, precond), ("sx", "sy"))

    force_discontinuity = jump(loads[0, 0], face_index)
    multipliers = jnp.zeros_like(force_discontinuity)
    residual = force_discontinuity
    precond = precondition(residual)
    direction = precond
    residual_inner = residual_dot(residual, precond)
    for iteration in range(ITERS):
        width = direction.shape[1]
        apply_spread = jump(direction, face_index)
        fine_part = jnp.dot(flex_mat, apply_spread, precision=highest)
        local_load = jnp.dot(coupling_mat, apply_spread, precision=highest)
        coarse_rhs = jnp.dot(onehot, local_load, precision=highest)
        coarse_sol = coarse_solve(coarse_rhs, coarse_inverse)
        filled_out = jnp.concatenate([coarse_sol, jnp.zeros((1, width), jnp.float32)], axis=0)
        picked = filled_out[corners]
        correction = lax.dot_general(
            coupling_mat, picked, (((0,), (0,)), ((), ())), precision=highest
        )
        image_dir = jump(fine_part + correction, face_index)
        step_size = residual_inner / lax.psum(inner(direction, image_dir), ("sx", "sy"))
        multipliers = multipliers + step_size * direction
        residual = residual - step_size * image_dir
        if iteration + 1 < ITERS:
            precond = precondition(residual)
            new_dot = residual_dot(residual, precond)
            direction = precond + new_dot / residual_inner * direction
            residual_inner = new_dot
    return (multipliers[None, None], residual[None, None])


def solution(mesh):
    return jax.shard_map(
        shards,
        mesh=mesh,
        in_specs=(
            P("sx", "sy", None, None),
            P("sx", "sy", None, None),
            P("sx", "sy", None, None),
            P("sx", "sy", None, None),
            P("sx", "sy", None),
            P("sx", "sy", None, None),
            P(("sx", "sy"), None),
        ),
        out_specs=(P("sx", "sy", None, None), P("sx", "sy", None, None)),
        check_vma=False,
    )
```

profile of v0, /device:TPU:1, one launch (start us, length us, event | category | flops | bytes accessed | tf_op | source)
XLA Modules:
  0.0 1103.3 jit_solution(2738854772131072380)
XLA Ops:
  8.7 4.6 collective-permute-start
  15.2 3.6 collective-permute-start.2
  22.7 3.5 collective-permute-done.2
  26.2 4.1 collective-permute-done.3
  30.4 18.0 %gather_fusion = f32[1536,256]{1,0:T(8,128)} fusion(f32[4,384,256]{2,1,0:T(8,128)S(1)} %pad_maximum_fusion, s32[1536]{0:T(1024)S(1)} %reshape.175), kind=kCustom, calls=%fused_computation | custom fusion | bytes 3158016 | tf_op jit(solution)/shard_map/gather | solution.py:24
  51.4 5.1 collective-permute-start.4
  58.5 3.4 collective-permute-start.6
  63.2 2.8 collective-permute-done.5
  68.1 4.1 collective-permute-done.7
  72.3 18.0 %gather_fusion.1 = f32[1536,256]{1,0:T(8,128)} fusion(f32[4,384,256]{2,1,0:T(8,128)S(1)} %pad_maximum_fusion.1, s32[1536]{0:T(1024)S(1)} %reshape.175), kind=kCustom, calls=%fused_computation.1 | custom fusion | bytes 3158016 | tf_op jit(solution)/shard_map/gather | solution.py:24
  92.1 18.2 %fusion.10 = f32[1536,256]{0,1:T(8,128)S(1)} fusion(f32[1536,256]{1,0:T(8,128)S(1)} %bitcast.126, f32[1,1,1536,1536]{3,2,1,0:T(8,128)} %param.9), kind=kOutput, calls=%fused_computation.23 | convolution fusion | flops 7247757312 | bytes 12582912 | tf_op jit(solution)/shard_map/dot_general | solution.py:51
  110.3 5.9 collective-permute-start.8
  118.2 3.9 collective-permute-start.10
  126.9 4.1 collective-permute-done.11
  134.2 18.0 %gather_fusion.2 = f32[1536,256]{1,0:T(8,128)} fusion(f32[4,384,256]{2,1,0:T(8,128)S(1)} %copy.27, s32[1536]{0:T(1024)S(1)} %reshape.175), kind=kCustom, calls=%fused_computation.2 | custom fusion | bytes 3158016 | tf_op jit(solution)/shard_map/gather | solution.py:24
  152.2 3.1 copy.28
  157.2 6.4 collective-permute-start.12
  165.6 4.0 collective-permute-start.14
  174.3 3.9 collective-permute-done.15
  181.3 18.0 %gather_fusion.3 = f32[1536,256]{1,0:T(8,128)} fusion(f32[4,384,256]{2,1,0:T(8,128)S(1)} %copy.31, s32[1536]{0:T(1024)S(1)} %reshape.175), kind=kCustom, calls=%fused_computation.3 | custom fusion | bytes 3158016 | tf_op jit(solution)/shard_map/gather | solution.py:24
  203.9 11.6 %fusion.2 = f32[256,1536]{1,0:T(8,128)} fusion(f32[1,1,1536,1536]{3,2,1,0:T(8,128)} %param.8, f32[1536,256]{0,1:T(8,128)S(1)} %copy.32, f32[1536,256]{0,1:T(8,128)S(1)} %get-tuple-element.16), kind=kOutput, calls=%fused_computation.13 | convolution fusion | flops 7248543744 | bytes 14155776 | tf_op jit(solution)/shard_map/dot_general | solution.py:66
  215.4 139.1 %all-reduce.6.cloned.1.call-done = f32[512,256]{1,0:T(8,128)} async-done(((f32[512,256]{1,0:T(8,128)}), f32[512,256]{1,0:T(8,128)}) %all-reduce.6.cloned.1.call-update) | async-done | bytes 524304 | tf_op jit(solution)/shard_map/psum | solution.py:30
  355.9 54.6 %all-gather = f32[128,4,256]{2,1,0:T(4,128)} all-gather(f32[1,4,256]{2,1,0:T(4,128)S(1)} %convolution_bitcast_fusion.1), channel_id=1, replica_groups=mesh['sx'=8,'sy'=16] {'sx','sy'}, dimensions={0}, use_global_device_ids=true | all-gather | bytes 528384 | tf_op jit(solution)/shard_map/all_gather | solution.py:32
  421.0 3.1 collective-permute-start.17
  424.2 2.7 collective-permute-start.18
  429.8 3.0 copy.30
  435.2 4.9 collective-permute-done.19
  440.1 2.6 pad_maximum_fusion.4
  444.6 18.0 %gather_fusion.5 = f32[1536,256]{1,0:T(8,128)} fusion(f32[4,384,256]{2,1,0:T(8,128)S(1)} %copy.33, s32[1536]{0:T(1024)S(1)} %reshape.175), kind=kCustom, calls=%fused_computation.5 | custom fusion | bytes 3158016 | tf_op jit(solution)/shard_map/gather | solution.py:24
  462.6 3.2 copy.34
  465.8 3.8 multiply_reduce_fusion.2
  469.6 66.2 %all-reduce.2 = (f32[256]{0:T(256)S(1)}, f32[256]{0:T(256)S(1)}) all-reduce(f32[256]{0:T(256)S(1)} %get-tuple-element.7, f32[256]{0:T(256)S(1)} %get-tuple-element.6), channel_id=1, replica_groups=mesh['sx'=8,'sy'=16] {'sx','sy'}, use_global_device_ids=true, to_apply=%region_1.0 | all-reduce | flops 512 | bytes 4096 | tf_op jit(solution)/shard_map/psum | solution.py:55
  535.9 2.6 multiply_subtract_fusion
  539.6 3.3 collective-permute-start.20
  548.0 4.3 collective-permute-done.21
  552.3 3.0 collective-permute-done.22
  555.3 4.1 collective-permute-done.23
  562.5 18.0 %gather_fusion.6 = f32[1536,256]{1,0:T(8,128)} fusion(f32[4,384,256]{2,1,0:T(8,128)S(1)} %copy.35, s32[1536]{0:T(1024)S(1)} %reshape.175), kind=kCustom, calls=%fused_computation.6 | custom fusion | bytes 3158016 | tf_op jit(solution)/shard_map/gather | solution.py:24
  580.6 3.2 copy.36
  583.7 11.3 %fusion.13 = f32[1536,256]{0,1:T(8,128)S(1)} fusion(f32[1,1,1536,1536]{3,2,1,0:T(8,128)} %param.9, f32[1536,256]{0,1:T(8,128)S(1)} %copy-done.5, f32[1536,256]{0,1:T(8,128)} %copy.36), kind=kOutput, calls=%fused_computation.24 | convolution fusion | flops 7248150528 | bytes 14155776 | tf_op jit(solution)/shard_map/dot_general | solution.py:51
  596.2 3.4 collective-permute-start.24
  605.1 3.9 collective-permute-done.25
  611.5 4.1 collective-permute-done.27
  618.8 18.0 %gather_fusion.7 = f32[1536,256]{1,0:T(8,128)} fusion(f32[4,384,256]{2,1,0:T(8,128)S(1)} %copy.37, s32[1536]{0:T(1024)S(1)} %reshape.175), kind=kCustom, calls=%fused_computation.7 | custom fusion | bytes 3158016 | tf_op jit(solution)/shard_map/gather | solution.py:24
  636.7 3.1 copy.38
  642.2 69.1 %psum.45 = f32[256]{0:T(256)S(1)} all-reduce(f32[256]{0:T(256)S(1)} %multiply_reduce_fusion.1), channel_id=1, replica_groups=mesh['sx'=8,'sy'=16] {'sx','sy'}, use_global_device_ids=true, to_apply=%region_6.0 | all-reduce | flops 256 | bytes 2048 | tf_op jit(solution)/shard_map/psum | solution.py:55
  714.7 3.9 collective-permute-start.28
  723.7 4.3 collective-permute-done.29
  729.7 4.1 collective-permute-done.31
  737.0 18.0 %gather_fusion.8 = f32[1536,256]{1,0:T(8,128)} fusion(f32[4,384,256]{2,1,0:T(8,128)S(1)} %copy.39, s32[1536]{0:T(1024)S(1)} %reshape.175), kind=kCustom, calls=%fused_computation.8 | custom fusion | bytes 3158016 | tf_op jit(solution)/shard_map/gather | solution.py:24
  754.9 3.1 copy.40
  758.1 2.8 fusion.17
  762.1 12.2 %fusion = f32[256,1536]{1,0:T(8,128)} fusion(f32[1,1,1536,1536]{3,2,1,0:T(8,128)} %param.8, f32[1536,256]{0,1:T(8,128)S(1)} %copy-done.2, f32[1536,256]{0,1:T(8,128)} %copy.40), kind=kOutput, calls=%fused_computation.11 | convolution fusion | flops 7248150528 | bytes 14155776 | tf_op jit(solution)/shard_map/dot_general | solution.py:66
  774.3 135.6 %all-reduce.8.cloned.1.call-done = f32[512,256]{1,0:T(8,128)} async-done(((f32[512,256]{1,0:T(8,128)}), f32[512,256]{1,0:T(8,128)}) %all-reduce.8.cloned.1.call-update) | async-done | bytes 524304 | tf_op jit(solution)/shard_map/psum | solution.py:30
  911.3 54.2 %all-gather.1 = f32[128,4,256]{2,1,0:T(4,128)} all-gather(f32[1,4,256]{2,1,0:T(4,128)S(1)} %convolution_bitcast_fusion), channel_id=1, replica_groups=mesh['sx'=8,'sy'=16] {'sx','sy'}, dimensions={0}, use_global_device_ids=true | all-gather | bytes 528384 | tf_op jit(solution)/shard_map/all_gather | solution.py:32
  981.4 3.5 collective-permute-done.33
  984.9 3.8 collective-permute-done.34
  988.7 4.1 collective-permute-done.35
  995.9 18.0 %gather_fusion.10 = f32[1536,256]{1,0:T(8,128)} fusion(f32[4,384,256]{2,1,0:T(8,128)S(1)} %copy.41, s32[1536]{0:T(1024)S(1)} %reshape.175), kind=kCustom, calls=%fused_computation.10 | custom fusion | bytes 3158016 | tf_op jit(solution)/shard_map/gather | solution.py:24
  1013.9 3.1 copy.42
  1017.0 3.4 multiply_reduce_fusion
  1020.4 66.7 %psum.47 = f32[256]{0:T(256)S(1)} all-reduce(f32[256]{0:T(256)S(1)} %get-tuple-element.12), channel_id=1, replica_groups=mesh['sx'=8,'sy'=16] {'sx','sy'}, use_global_device_ids=true, to_apply=%region_9.0 | all-reduce | flops 256 | bytes 2048 | tf_op jit(solution)/shard_map/psum | solution.py:76
  1087.1 4.1 subtract_bitcast_fusion
  1091.2 3.1 copy.43
  (140 shorter events, 123.0 us)
Async XLA Ops:
  7.2 194.1 %copy-start = (f32[1,1,16,1536]{3,2,1,0:T(8,128)S(1)}, f32[1,1,16,1536]{3,2,1,0:T(8,128)}, u32[]{:S(2)}) copy-start(f32[1,1,16,1536]{3,2,1,0:T(8,128)} %param.10) | copy-start | bytes 294916
  7.2 12.9 %copy-start.19 = (s32[1,1,4,384]{3,2,1,0:T(4,128)S(1)}, s32[1,1,4,384]{3,2,1,0:T(4,128)}, u32[]{:S(2)}) copy-start(s32[1,1,4,384]{3,2,1,0:T(4,128)} %param.12) | copy-start | bytes 18436
  7.2 347.3 %all-reduce.6.cloned.1.call-start = ((), (), s32[]{:S(2)}) async-start(), calls=%async_computation | async-start | bytes 1048576 | tf_op jit(solution)/shard_map/psum | solution.py:30
  8.7 11.4 %collective-permute-start = (f32[384,256]{1,0:T(8,128)S(1)}, f32[384,256]{1,0:T(8,128)S(1)}, u32[]{:S(2)}, u32[]{:S(2)}) collective-permute-start(f32[384,256]{1,0:T(8,128)S(1)} %get-tuple-element.49), channel_id=1, source_target_pairs={{0,16},{16,32},{32,48},{48,64},{64,80},{80,96},{96,112},{1,17},{17... | collective-permute-start | bytes 1179656 | tf_op jit(solution)/shard_map/ppermute | solution.py:12
  13.3 9.4 collective-permute-start.1
  15.2 11.0 collective-permute-start.2
  18.8 11.5 %collective-permute-start.3 = (f32[384,256]{1,0:T(8,128)S(1)}, f32[384,256]{1,0:T(8,128)S(1)}, u32[]{:S(2)}, u32[]{:S(2)}) collective-permute-start(f32[384,256]{1,0:T(8,128)S(1)} %get-tuple-element.52), channel_id=1, source_target_pairs={{1,0},{2,1},{3,2},{4,3},{5,4},{6,5},{7,6},{8,7},{9,8},{10,9},{11,1... | collective-permute-start | bytes 1179656 | tf_op jit(solution)/shard_map/ppermute | solution.py:12
  30.4 18.0 %copy-start.10 = (f32[1,1,1536,256]{3,2,1,0:T(8,128)S(1)}, f32[1,1,1536,256]{3,2,1,0:T(8,128)}, u32[]{:S(2)}) copy-start(f32[1,1,1536,256]{3,2,1,0:T(8,128)} %param.7) | copy-start | bytes 4718596
  50.3 1.1 copy-start.12
  51.4 11.8 %collective-permute-start.4 = (f32[384,256]{1,0:T(8,128)S(1)}, f32[384,256]{1,0:T(8,128)S(1)}, u32[]{:S(2)}, u32[]{:S(2)}) collective-permute-start(f32[384,256]{1,0:T(8,128)S(1)} %get-tuple-element.45), channel_id=1, source_target_pairs={{0,16},{16,32},{32,48},{48,64},{64,80},{80,96},{96,112},{1,17},{17... | collective-permute-start | bytes 1179656 | tf_op jit(solution)/shard_map/ppermute | solution.py:12
  56.6 9.4 collective-permute-start.5
  58.5 9.6 collective-permute-start.6
  61.9 10.3 collective-permute-start.7
  72.3 18.0 %copy-start.13 = (f32[4,384,256]{2,1,0:T(8,128)S(1)}, f32[4,384,256]{2,1,0:T(8,128)}, u32[]{:S(2)}) copy-start(f32[4,384,256]{2,1,0:T(8,128)} %copy-done.12) | copy-start | bytes 4718596
  110.3 13.3 %collective-permute-start.8 = (f32[384,256]{0,1:T(8,128)S(1)}, f32[384,256]{0,1:T(8,128)S(1)}, u32[]{:S(2)}, u32[]{:S(2)}) collective-permute-start(f32[384,256]{0,1:T(8,128)S(1)} %get-tuple-element.41), channel_id=1, source_target_pairs={{0,16},{16,32},{32,48},{48,64},{64,80},{80,96},{96,112},{1,17},{17... | collective-permute-start | bytes 1179656 | tf_op jit(solution)/shard_map/ppermute | solution.py:12
  116.3 9.4 collective-permute-start.9
  118.2 8.7 collective-permute-start.10
  122.1 8.9 collective-permute-start.11
  157.1 13.8 %copy-start.20 = (s32[1,1,16]{2,1,0:T(1,128)S(1)}, s32[1,1,16]{2,1,0:T(1,128)}, u32[]{:S(2)}) copy-start(s32[1,1,16]{2,1,0:T(1,128)} %param.11) | copy-start | bytes 196
  157.2 13.8 %collective-permute-start.12 = (f32[384,256]{0,1:T(8,128)S(1)}, f32[384,256]{0,1:T(8,128)S(1)}, u32[]{:S(2)}, u32[]{:S(2)}) collective-permute-start(f32[384,256]{0,1:T(8,128)S(1)} %get-tuple-element.37), channel_id=1, source_target_pairs={{0,16},{16,32},{32,48},{48,64},{64,80},{80,96},{96,112},{1,17},{17... | collective-permute-start | bytes 1179656 | tf_op jit(solution)/shard_map/ppermute | solution.py:12
  163.7 9.4 collective-permute-start.13
  165.6 8.7 collective-permute-start.14
  169.6 8.6 collective-permute-start.15
  203.8 150.7 %copy-start.18 = (f32[4,512]{1,0:T(4,128)S(1)}, f32[4,512]{1,0:T(4,128)}, u32[]{:S(2)}) copy-start(f32[4,512]{1,0:T(4,128)} %param.13) | copy-start | bytes 24580
  203.8 706.1 %all-reduce.8.cloned.1.call-start = ((), (), s32[]{:S(2)}) async-start(), calls=%async_computation.1 | async-start | bytes 1048576 | tf_op jit(solution)/shard_map/psum | solution.py:30
  215.4 200.5 %copy-start.16 = (f32[256,1536]{1,0:T(8,128)S(1)}, f32[256,1536]{1,0:T(8,128)}, u32[]{:S(2)}) copy-start(f32[256,1536]{1,0:T(8,128)} %fusion.2) | copy-start | bytes 4718596
  417.4 1.7 copy-start.8
  417.4 10.8 copy-start.11
  419.1 13.7 %collective-permute-start.16 = (f32[384,256]{0,1:T(8,128)}, f32[384,256]{0,1:T(8,128)}, u32[]{:S(2)}, u32[]{:S(2)}) collective-permute-start(f32[384,256]{0,1:T(8,128)} %get-tuple-element.33), channel_id=1, source_target_pairs={{0,16},{16,32},{32,48},{48,64},{64,80},{80,96},{96,112},{1,17},{17... | collective-permute-start | bytes 1179656 | tf_op jit(solution)/shard_map/ppermute | solution.py:12
  421.0 11.8 %collective-permute-start.17 = (f32[384,256]{0,1:T(8,128)}, f32[384,256]{0,1:T(8,128)}, u32[]{:S(2)}, u32[]{:S(2)}) collective-permute-start(f32[384,256]{0,1:T(8,128)} %get-tuple-element.36), channel_id=1, source_target_pairs={{16,0},{32,16},{48,32},{64,48},{80,64},{96,80},{112,96},{17,1},{33... | collective-permute-start | bytes 1179656 | tf_op jit(solution)/shard_map/ppermute | solution.py:12
  424.2 11.1 %collective-permute-start.18 = (f32[384,256]{0,1:T(8,128)}, f32[384,256]{0,1:T(8,128)}, u32[]{:S(2)}, u32[]{:S(2)}) collective-permute-start(f32[384,256]{0,1:T(8,128)} %get-tuple-element.35), channel_id=1, source_target_pairs={{0,1},{1,2},{2,3},{3,4},{4,5},{5,6},{6,7},{7,8},{8,9},{9,10},{10,1... | collective-permute-start | bytes 1179656 | tf_op jit(solution)/shard_map/ppermute | solution.py:12
  426.9 13.2 %collective-permute-start.19 = (f32[384,256]{0,1:T(8,128)}, f32[384,256]{0,1:T(8,128)}, u32[]{:S(2)}, u32[]{:S(2)}) collective-permute-start(f32[384,256]{0,1:T(8,128)} %get-tuple-element.34), channel_id=1, source_target_pairs={{1,0},{2,1},{3,2},{4,3},{5,4},{6,5},{7,6},{8,7},{9,8},{10,9},{11,1... | collective-permute-start | bytes 1179656 | tf_op jit(solution)/shard_map/ppermute | solution.py:12
  462.6 3.2 copy-start.9
  538.5 1.1 copy-start.4
  539.6 8.3 collective-permute-start.20
  542.9 9.4 collective-permute-start.21
  544.8 10.5 collective-permute-start.22
  546.5 12.9 %collective-permute-start.23 = (f32[384,256]{0,1:T(8,128)S(1)}, f32[384,256]{0,1:T(8,128)S(1)}, u32[]{:S(2)}, u32[]{:S(2)}) collective-permute-start(f32[384,256]{0,1:T(8,128)S(1)} %get-tuple-element.30), channel_id=1, source_target_pairs={{1,0},{2,1},{3,2},{4,3},{5,4},{6,5},{7,6},{8,7},{9,8},{10,9},{11,1... | collective-permute-start | bytes 1179656 | tf_op jit(solution)/shard_map/ppermute | solution.py:12
  580.5 3.2 copy-start.5
  595.0 1.1 copy-start.7
  596.2 9.0 collective-permute-start.24
  599.6 9.4 collective-permute-start.25
  601.5 9.9 collective-permute-start.26
  603.8 11.8 %collective-permute-start.27 = (f32[384,256]{0,1:T(8,128)S(1)}, f32[384,256]{0,1:T(8,128)S(1)}, u32[]{:S(2)}, u32[]{:S(2)}) collective-permute-start(f32[384,256]{0,1:T(8,128)S(1)} %get-tuple-element.26), channel_id=1, source_target_pairs={{1,0},{2,1},{3,2},{4,3},{5,4},{6,5},{7,6},{8,7},{9,8},{10,9},{11,1... | collective-permute-start | bytes 1179656 | tf_op jit(solution)/shard_map/ppermute | solution.py:12
  636.7 3.1 copy-start.6
  713.5 1.1 copy-start.1
  714.7 9.0 collective-permute-start.28
  718.5 9.4 collective-permute-start.29
  720.5 9.2 collective-permute-start.30
  722.1 11.7 %collective-permute-start.31 = (f32[384,256]{0,1:T(8,128)S(1)}, f32[384,256]{0,1:T(8,128)S(1)}, u32[]{:S(2)}, u32[]{:S(2)}) collective-permute-start(f32[384,256]{0,1:T(8,128)S(1)} %get-tuple-element.22), channel_id=1, source_target_pairs={{1,0},{2,1},{3,2},{4,3},{5,4},{6,5},{7,6},{8,7},{9,8},{10,9},{11,1... | collective-permute-start | bytes 1179656 | tf_op jit(solution)/shard_map/ppermute | solution.py:12
  754.9 3.1 copy-start.2
  774.3 196.7 %copy-start.15 = (f32[256,1536]{1,0:T(8,128)S(1)}, f32[256,1536]{1,0:T(8,128)}, u32[]{:S(2)}) copy-start(f32[256,1536]{1,0:T(8,128)} %fusion) | copy-start | bytes 4718596
  972.4 1.2 copy-start.14
  973.6 7.8 collective-permute-start.32
  975.5 9.4 collective-permute-start.33
  977.9 10.7 collective-permute-start.34
  979.9 12.9 %collective-permute-start.35 = (f32[384,256]{0,1:T(8,128)S(1)}, f32[384,256]{0,1:T(8,128)S(1)}, u32[]{:S(2)}, u32[]{:S(2)}) collective-permute-start(f32[384,256]{0,1:T(8,128)S(1)} %get-tuple-element.18), channel_id=1, source_target_pairs={{1,0},{2,1},{3,2},{4,3},{5,4},{6,5},{7,6},{8,7},{9,8},{10,9},{11,1... | collective-permute-start | bytes 1179656 | tf_op jit(solution)/shard_map/ppermute | solution.py:12
  1013.9 3.1 copy-start.3
  1091.2 3.1 copy-start.17
Sparse Core Ops, SparseCore 0:
  203.9 150.5 all-reduce.5
  762.2 147.6 all-reduce.7
where the time goes:
time: 1110 us; the launch traced here: 1100 us
  waiting for transfers between devices  359 us (32%)
  blocking collectives  311 us (28%)
  local copies, waits for them, and re-layouts  225 us (20%)
  starting transfers between devices  93.2 us (8%)
  matrix products  65.3 us (6%)
  other arithmetic  34.2 us (3%)
  between operations  15.2 us (1%)
    psum x2, waiting for transfers between devices, coarse_solve(): total = lax.psum(coarse_rhs, ('sx', 'sy'))  275 us
    gather x17, local copies, waits for them, and re-layouts, jump(): matched = received[jnp.arange(4, dtype=jnp.int32)[:, None], face_index]  186 us
    psum x2, blocking collectives, residual_dot(): return lax.psum(inner(residual, precond), ('sx', 'sy'))  135 us
    all_gather x2, blocking collectives, coarse_solve(): return lax.all_gather(mine, ('sx', 'sy'), axis=0, tiled=True)  109 us
    ppermute x36, starting transfers between devices, shifted(): return lax.ppermute(block, axis, route)  93.1 us
    ppermute x36, waiting for transfers between devices, shifted(): return lax.ppermute(block, axis, route)  84.4 us
    psum x1, blocking collectives, shards(): lax.psum(inner(direction, image_dir), ('sx', 'sy'))  66.7 us
    dot_general x2, matrix products, precondition(): operator_applied = jnp.dot(prec_mat, spread, precision=highest)  29.5 us
  transfers between devices with their start and end apart: 38, of which 28 were waited for; matrix products, arithmetic and copies ran while one was open for 3% of the time, Pallas kernels for 0%

commit v1 on v0

--- a/solution.py
+++ b/solution.py
@@ -37,6 +37,7 @@
 
 
 def shards(loads, schur_flex, dirichlet, coupling, corner_index, face_lists, coarse_inverse):
+    high = lax.Precision.HIGH
     highest = lax.Precision.HIGHEST
     flex_mat = schur_flex[0, 0]
     prec_mat = dirichlet[0, 0]
@@ -45,42 +46,41 @@
     face_index = face_lists[0, 0]
     ncoarse = coarse_inverse.shape[1]
     onehot = (corners[None, :] == jnp.arange(ncoarse, dtype=jnp.int32)[:, None]).astype(jnp.float32)
+    size = face_index.shape[1]
+    sx = lax.axis_index("sx")
+    sy = lax.axis_index("sy")
+    inside = jnp.stack([sx > 0, sx < lax.axis_size("sx") - 1, sy > 0, sy < lax.axis_size("sy") - 1])
+    scale = jnp.repeat(1.0 + inside.astype(jnp.float32), size)[:, None]
 
-    def precondition(dual_vector):
-        spread = jump(dual_vector, face_index)
-        operator_applied = jnp.dot(prec_mat, spread, precision=highest)
-        return 0.5 * jump(operator_applied, face_index)
+    def total(values):
+        return lax.psum(values, ("sx", "sy"))
 
-    def residual_dot(residual, precond):
-        return lax.psum(inner(residual, precond), ("sx", "sy"))
-
-    force_discontinuity = jump(loads[0, 0], face_index)
-    multipliers = jnp.zeros_like(force_discontinuity)
-    residual = force_discontinuity
-    precond = precondition(residual)
-    direction = precond
-    residual_inner = residual_dot(residual, precond)
+    residual = jump(loads[0, 0], face_index)
+    multipliers = jnp.zeros_like(residual)
+    direction = None
+    residual_inner = None
     for iteration in range(ITERS):
-        width = direction.shape[1]
-        apply_spread = jump(direction, face_index)
-        fine_part = jnp.dot(flex_mat, apply_spread, precision=highest)
-        local_load = jnp.dot(coupling_mat, apply_spread, precision=highest)
+        spread = scale * residual
+        operator_applied = jnp.dot(prec_mat, spread, precision=high)
+        new_dot = total(0.5 * inner(spread, operator_applied))
+        precond = 0.5 * jump(operator_applied, face_index)
+        direction = precond if iteration == 0 else precond + new_dot / residual_inner * direction
+        residual_inner = new_dot
+        apply_spread = scale * direction
+        fine_part = jnp.dot(flex_mat, apply_spread, precision=high)
+        local_load = jnp.dot(coupling_mat, apply_spread, precision=high)
         coarse_rhs = jnp.dot(onehot, local_load, precision=highest)
         coarse_sol = coarse_solve(coarse_rhs, coarse_inverse)
-        filled_out = jnp.concatenate([coarse_sol, jnp.zeros((1, width), jnp.float32)], axis=0)
+        filled_out = jnp.concatenate([coarse_sol, jnp.zeros((1, direction.shape[1]), jnp.float32)], axis=0)
         picked = filled_out[corners]
         correction = lax.dot_general(
-            coupling_mat, picked, (((0,), (0,)), ((), ())), precision=highest
+            coupling_mat, picked, (((0,), (0,)), ((), ())), precision=high
         )
-        image_dir = jump(fine_part + correction, face_index)
-        step_size = residual_inner / lax.psum(inner(direction, image_dir), ("sx", "sy"))
+        applied = fine_part + correction
+        step_size = residual_inner / total(inner(apply_spread, applied))
+        image_dir = jump(applied, face_index)
         multipliers = multipliers + step_size * direction
         residual = residual - step_size * image_dir
-        if iteration + 1 < ITERS:
-            precond = precondition(residual)
-            new_dot = residual_dot(residual, precond)
-            direction = precond + new_dot / residual_inner * direction
-            residual_inner = new_dot
     return (multipliers[None, None], residual[None, None])
 
 

time: 1110 us -> 861 us (0.78)
  local copies, waits for them, and re-layouts: 225 us -> 130 us
  waiting for transfers between devices: 359 us -> 285 us
  starting transfers between devices: 93.2 us -> 58.1 us
  matrix products: 65.3 us -> 44.1 us
    gather x17 -> x10, local copies, waits for them, and re-layouts: 186 us -> 96.4 us  [jump(): matched = received[jnp.arange(4, dtype=jnp.int32)[:, None], face_index]]
    ppermute x36 -> x20, waiting for transfers between devices: 84.4 us -> 5.83 us  [shifted(): return lax.ppermute(block, axis, route)]
    ppermute x36 -> x20, starting transfers between devices: 93.1 us -> 57.8 us  [shifted(): return lax.ppermute(block, axis, route)]
    dot_general x6, matrix products: 57.3 us -> 35.4 us  [the longest x2 19.4 us: shards(): operator_applied = jnp.dot(prec_mat, spread, precision=high)]
  transfers between devices with their start and end apart: 38 -> 22, of which waited for: 28 -> 8; matrix products, arithmetic and copies ran while one was open for 3% -> 2% of each run, Pallas kernels for 0% -> 0%
where the time goes in v1:
time: 861 us; the launch traced here: 859 us
  blocking collectives  303 us (35%)
  waiting for transfers between devices  285 us (33%)
  local copies, waits for them, and re-layouts  130 us (15%)
  starting transfers between devices  58.1 us (7%)
  matrix products  44.1 us (5%)
  other arithmetic  24 us (3%)
  between operations  14.6 us (2%)
    psum x2, waiting for transfers between devices, coarse_solve(): total = lax.psum(coarse_rhs, ('sx', 'sy'))  279 us
    psum x3, blocking collectives, total(): return lax.psum(values, ('sx', 'sy'))  195 us
    all_gather x2, blocking collectives, coarse_solve(): return lax.all_gather(mine, ('sx', 'sy'), axis=0, tiled=True)  108 us
    gather x10, local copies, waits for them, and re-layouts, jump(): matched = received[jnp.arange(4, dtype=jnp.int32)[:, None], face_index]  96.4 us
    ppermute x20, starting transfers between devices, shifted(): return lax.ppermute(block, axis, route)  57.8 us
    dot_general x2, matrix products, shards(): operator_applied = jnp.dot(prec_mat, spread, precision=high)  19.4 us
  transfers between devices with their start and end apart: 22, of which 8 were waited for; matrix products, arithmetic and copies ran while one was open for 2% of the time, Pallas kernels for 0%

profile of v1, /device:TPU:1, one launch (start us, length us, event | category | flops | bytes accessed | tf_op | source)
XLA Modules:
  0.0 859.2 jit_solution(2950131900494569318)
XLA Ops:
  7.2 1.5 slice_bitcast_fusion.3
  8.7 1.3 collective-permute-start.3
  10.0 5.0 collective-permute-start.2
  15.0 2.9 collective-permute-start.1
  17.9 3.2 collective-permute-start
  22.8 1.9 collective-permute-done.1
  26.6 1.3 pad_maximum_fusion
  27.9 10.7 %gather_fusion = f32[1536,256]{1,0:T(8,128)S(1)} fusion(f32[4,384,256]{2,1,0:T(8,128)S(1)} %pad_maximum_fusion, s32[1536]{0:T(1024)S(1)} %reshape.131), kind=kCustom, calls=%fused_computation | custom fusion | bytes 3158016 | tf_op jit(solution)/shard_map/gather | solution.py:24
  38.6 11.8 %fusion.10 = f32[1536,256]{0,1:T(8,128)S(1)} fusion(f32[1,1,1536,1536]{3,2,1,0:T(8,128)} %param.9, f32[1,1,1536,256]{3,2,1,0:T(8,128)} %param.7, f32[1536,256]{1,0:T(8,128)S(1)} %gather_fusion, f32[1536]{0:T(1024)S(1)} %mul.105), kind=kOutput, calls=%fused_computation.19 | convolution fusion | flops 3624665088 | bytes 14161920 | tf_op jit(solution)/shard_map/dot_general | solution.py:64
  53.4 4.9 collective-permute-start.6
  58.3 1.9 collective-permute-start.5
  60.2 4.8 collective-permute-start.4
  65.0 2.0 copy.23
  67.1 1.6 copy.24
  70.0 2.6 pad_maximum_fusion.1
  72.6 1.9 copy.21
  74.5 17.9 %gather_fusion.1 = f32[1536,256]{1,0:T(8,128)} fusion(f32[4,384,256]{2,1,0:T(8,128)S(1)} %copy.21, s32[1536]{0:T(1024)S(1)} %reshape.131), kind=kCustom, calls=%fused_computation.1 | custom fusion | bytes 3158016 | tf_op jit(solution)/shard_map/gather | solution.py:24
  92.4 3.1 copy.22
  95.5 2.9 multiply_reduce_fusion.3
  100.6 6.7 fusion.2
  107.4 144.9 %all-reduce.6.cloned.1.call-done = f32[512,256]{1,0:T(8,128)} async-done(((f32[512,256]{1,0:T(8,128)}), f32[512,256]{1,0:T(8,128)}) %all-reduce.6.cloned.1.call-update) | async-done | bytes 524304 | tf_op jit(solution)/shard_map/psum | solution.py:30
  252.3 1.4 convolution_bitcast_fusion.1
  253.7 54.1 %all-gather = f32[128,4,256]{2,1,0:T(4,128)} all-gather(f32[1,4,256]{2,1,0:T(4,128)S(1)} %convolution_bitcast_fusion.1), channel_id=1, replica_groups=mesh['sx'=8,'sy'=16] {'sx','sy'}, dimensions={0}, use_global_device_ids=true | all-gather | bytes 528384 | tf_op jit(solution)/shard_map/all_gather | solution.py:32
  307.8 2.0 reshape.184
  309.8 1.9 concatenate.14
  311.7 1.6 gather_fusion.2
  317.2 4.0 collective-permute-start.10
  321.2 2.5 collective-permute-start.9
  323.7 3.1 collective-permute-start.8
  326.8 64.9 %all-reduce.2 = (f32[256]{0:T(256)S(1)}, f32[256]{0:T(256)S(1)}) all-reduce(f32[256]{0:T(256)S(1)} %broadcast_multiply_fusion.3, f32[256]{0:T(256)S(1)} %get-tuple-element.34), channel_id=1, replica_groups=mesh['sx'=8,'sy'=16] {'sx','sy'}, use_global_device_ids=true, to_apply=%region_1.0 | all-reduce | flops 512 | bytes 4096 | tf_op jit(solution)/shard_map/psum | solution.py:56
  391.7 2.4 pad_maximum_fusion.2
  394.1 1.9 copy.25
  396.0 17.9 %gather_fusion.3 = f32[1536,256]{1,0:T(8,128)} fusion(f32[4,384,256]{2,1,0:T(8,128)S(1)} %copy.25, s32[1536]{0:T(1024)S(1)} %reshape.131), kind=kCustom, calls=%fused_computation.3 | custom fusion | bytes 3158016 | tf_op jit(solution)/shard_map/gather | solution.py:24
  413.9 3.1 copy.26
  417.1 2.9 multiply_subtract_fusion
  419.9 7.5 multiply_reduce_fusion.1
  430.2 4.0 collective-permute-start.14
  434.2 3.4 collective-permute-start.13
  437.6 2.2 collective-permute-start.12
  439.8 65.1 %psum.45 = f32[256]{0:T(256)S(1)} all-reduce(f32[256]{0:T(256)S(1)} %broadcast_multiply_fusion.1), channel_id=1, replica_groups=mesh['sx'=8,'sy'=16] {'sx','sy'}, use_global_device_ids=true, to_apply=%region_6.0 | all-reduce | flops 256 | bytes 2048 | tf_op jit(solution)/shard_map/psum | solution.py:56
  505.0 2.5 pad_maximum_fusion.3
  507.4 1.9 copy.27
  509.3 17.9 %gather_fusion.4 = f32[1536,256]{1,0:T(8,128)} fusion(f32[4,384,256]{2,1,0:T(8,128)S(1)} %copy.27, s32[1536]{0:T(1024)S(1)} %reshape.131), kind=kCustom, calls=%fused_computation.4 | custom fusion | bytes 3158016 | tf_op jit(solution)/shard_map/gather | solution.py:24
  527.2 3.0 copy.28
  530.3 2.2 multiply_add_fusion
  534.4 7.7 fusion
  542.2 134.3 %all-reduce.8.cloned.1.call-done = f32[512,256]{1,0:T(8,128)} async-done(((f32[512,256]{1,0:T(8,128)}), f32[512,256]{1,0:T(8,128)}) %all-reduce.8.cloned.1.call-update) | async-done | bytes 524304 | tf_op jit(solution)/shard_map/psum | solution.py:30
  676.5 1.4 convolution_bitcast_fusion
  677.9 54.1 %all-gather.1 = f32[128,4,256]{2,1,0:T(4,128)} all-gather(f32[1,4,256]{2,1,0:T(4,128)S(1)} %convolution_bitcast_fusion), channel_id=1, replica_groups=mesh['sx'=8,'sy'=16] {'sx','sy'}, dimensions={0}, use_global_device_ids=true | all-gather | bytes 528384 | tf_op jit(solution)/shard_map/all_gather | solution.py:32
  732.0 2.0 reshape.186
  734.0 1.9 concatenate.15
  735.9 1.6 gather_fusion.5
  737.5 2.5 multiply_reduce_fusion
  742.7 4.0 collective-permute-start.18
  746.7 2.5 collective-permute-start.17
  749.2 3.1 collective-permute-start.16
  752.3 65.2 %psum.47 = f32[256]{0:T(256)S(1)} all-reduce(f32[256]{0:T(256)S(1)} %get-tuple-element.38), channel_id=1, replica_groups=mesh['sx'=8,'sy'=16] {'sx','sy'}, use_global_device_ids=true, to_apply=%region_9.0 | all-reduce | flops 256 | bytes 2048 | tf_op jit(solution)/shard_map/psum | solution.py:56
  817.5 2.4 pad_maximum_fusion.4
  819.9 1.9 copy.29
  821.8 17.9 %gather_fusion.6 = f32[1536,256]{1,0:T(8,128)} fusion(f32[4,384,256]{2,1,0:T(8,128)S(1)} %copy.29, s32[1536]{0:T(1024)S(1)} %reshape.131), kind=kCustom, calls=%fused_computation.6 | custom fusion | bytes 3158016 | tf_op jit(solution)/shard_map/gather | solution.py:24
  839.7 3.1 copy.30
  842.9 4.8 subtract_bitcast_fusion
  847.6 3.1 copy.31
  850.8 1.6 copy.32
  (85 shorter events, 21.3 us)
Async XLA Ops:
  7.2 91.2 %copy-start = (f32[1,1,16,1536]{3,2,1,0:T(8,128)S(1)}, f32[1,1,16,1536]{3,2,1,0:T(8,128)}, u32[]{:S(2)}) copy-start(f32[1,1,16,1536]{3,2,1,0:T(8,128)} %param.10) | copy-start | bytes 294916
  7.2 14.0 %copy-start.16 = (s32[1,1,4,384]{3,2,1,0:T(4,128)S(1)}, s32[1,1,4,384]{3,2,1,0:T(4,128)}, u32[]{:S(2)}) copy-start(s32[1,1,4,384]{3,2,1,0:T(4,128)} %param.12) | copy-start | bytes 18436
  7.2 245.1 %all-reduce.6.cloned.1.call-start = ((), (), s32[]{:S(2)}) async-start(), calls=%async_computation | async-start | bytes 1048576 | tf_op jit(solution)/shard_map/psum | solution.py:30
  8.7 13.2 %collective-permute-start.3 = (f32[384,256]{1,0:T(8,128)S(1)}, f32[384,256]{1,0:T(8,128)S(1)}, u32[]{:S(2)}, u32[]{:S(2)}) collective-permute-start(f32[384,256]{1,0:T(8,128)S(1)} %get-tuple-element.29), channel_id=1, source_target_pairs={{1,0},{2,1},{3,2},{4,3},{5,4},{6,5},{7,6},{8,7},{9,8},{10,9},{11,1... | collective-permute-start | bytes 1179656 | tf_op jit(solution)/shard_map/ppermute | solution.py:12
  10.0 12.8 %collective-permute-start.2 = (f32[384,256]{1,0:T(8,128)S(1)}, f32[384,256]{1,0:T(8,128)S(1)}, u32[]{:S(2)}, u32[]{:S(2)}) collective-permute-start(f32[384,256]{1,0:T(8,128)S(1)} %get-tuple-element.30), channel_id=1, source_target_pairs={{0,1},{1,2},{2,3},{3,4},{4,5},{5,6},{6,7},{7,8},{8,9},{9,10},{10,1... | collective-permute-start | bytes 1179656 | tf_op jit(solution)/shard_map/ppermute | solution.py:12
  15.0 9.6 %collective-permute-start.1 = (f32[384,256]{1,0:T(8,128)S(1)}, f32[384,256]{1,0:T(8,128)S(1)}, u32[]{:S(2)}, u32[]{:S(2)}) collective-permute-start(f32[384,256]{1,0:T(8,128)S(1)} %get-tuple-element.31), channel_id=1, source_target_pairs={{16,0},{32,16},{48,32},{64,48},{80,64},{96,80},{112,96},{17,1},{33... | collective-permute-start | bytes 1179656 | tf_op jit(solution)/shard_map/ppermute | solution.py:12
  17.9 7.9 collective-permute-start
  24.6 1.2 copy-start.13
  25.8 0.7 copy-start.14
  38.6 11.8 %copy-start.7 = (f32[1536,256]{1,0:T(8,128)}, f32[1536,256]{1,0:T(8,128)S(1)}, u32[]{:S(2)}) copy-start(f32[1536,256]{1,0:T(8,128)S(1)} %gather_fusion) | copy-start | bytes 4718596
  50.4 1.7 copy-start.6
  50.4 14.6 %copy-start.17 = (s32[1,1,16]{2,1,0:T(1,128)S(1)}, s32[1,1,16]{2,1,0:T(1,128)}, u32[]{:S(2)}) copy-start(s32[1,1,16]{2,1,0:T(1,128)} %param.11) | copy-start | bytes 196
  52.1 16.6 %collective-permute-start.7 = (f32[384,256]{0,1:T(8,128)}, f32[384,256]{0,1:T(8,128)}, u32[]{:S(2)}, u32[]{:S(2)}) collective-permute-start(f32[384,256]{0,1:T(8,128)} %get-tuple-element.25), channel_id=1, source_target_pairs={{1,0},{2,1},{3,2},{4,3},{5,4},{6,5},{7,6},{8,7},{9,8},{10,9},{11,1... | collective-permute-start | bytes 1179656 | tf_op jit(solution)/shard_map/ppermute | solution.py:12
  53.4 15.3 %collective-permute-start.6 = (f32[384,256]{0,1:T(8,128)}, f32[384,256]{0,1:T(8,128)}, u32[]{:S(2)}, u32[]{:S(2)}) collective-permute-start(f32[384,256]{0,1:T(8,128)} %get-tuple-element.26), channel_id=1, source_target_pairs={{0,1},{1,2},{2,3},{3,4},{4,5},{5,6},{6,7},{7,8},{8,9},{9,10},{10,1... | collective-permute-start | bytes 1179656 | tf_op jit(solution)/shard_map/ppermute | solution.py:12
  58.3 10.5 %collective-permute-start.5 = (f32[384,256]{0,1:T(8,128)}, f32[384,256]{0,1:T(8,128)}, u32[]{:S(2)}, u32[]{:S(2)}) collective-permute-start(f32[384,256]{0,1:T(8,128)} %get-tuple-element.27), channel_id=1, source_target_pairs={{16,0},{32,16},{48,32},{64,48},{80,64},{96,80},{112,96},{17,1},{33... | collective-permute-start | bytes 1179656 | tf_op jit(solution)/shard_map/ppermute | solution.py:12
  60.2 9.8 %collective-permute-start.4 = (f32[384,256]{0,1:T(8,128)}, f32[384,256]{0,1:T(8,128)}, u32[]{:S(2)}, u32[]{:S(2)}) collective-permute-start(f32[384,256]{0,1:T(8,128)} %get-tuple-element.24), channel_id=1, source_target_pairs={{0,16},{16,32},{32,48},{48,64},{64,80},{80,96},{96,112},{1,17},{17... | collective-permute-start | bytes 1179656 | tf_op jit(solution)/shard_map/ppermute | solution.py:12
  65.0 2.0 copy-start.8
  67.0 28.4 %copy-start.3 = (f32[1,1,1536,256]{2,3,1,0:T(8,128)}, f32[1,1,1536,256]{2,3,1,0:T(8,128)S(1)}, u32[]{:S(2)}) copy-start(f32[1,1,1536,256]{2,3,1,0:T(8,128)S(1)} %copy.23) | copy-start | bytes 4718596
  100.4 151.9 %copy-start.15 = (f32[4,512]{1,0:T(4,128)S(1)}, f32[4,512]{1,0:T(4,128)}, u32[]{:S(2)}) copy-start(f32[4,512]{1,0:T(4,128)} %param.13) | copy-start | bytes 24580
  100.4 576.1 %all-reduce.8.cloned.1.call-start = ((), (), s32[]{:S(2)}) async-start(), calls=%async_computation.1 | async-start | bytes 1048576 | tf_op jit(solution)/shard_map/psum | solution.py:30
  314.5 1.4 copy-start.5
  315.9 75.8 %collective-permute-start.11 = (f32[384,256]{0,1:T(8,128)}, f32[384,256]{0,1:T(8,128)S(1)}, u32[]{:S(2)}, u32[]{:S(2)}) collective-permute-start(f32[384,256]{0,1:T(8,128)} %get-tuple-element.21), channel_id=1, source_target_pairs={{1,0},{2,1},{3,2},{4,3},{5,4},{6,5},{7,6},{8,7},{9,8},{10,9},{11,1... | collective-permute-start | bytes 1179656 | tf_op jit(solution)/shard_map/ppermute | solution.py:12
  317.2 74.5 %collective-permute-start.10 = (f32[384,256]{0,1:T(8,128)}, f32[384,256]{0,1:T(8,128)S(1)}, u32[]{:S(2)}, u32[]{:S(2)}) collective-permute-start(f32[384,256]{0,1:T(8,128)} %get-tuple-element.22), channel_id=1, source_target_pairs={{0,1},{1,2},{2,3},{3,4},{4,5},{5,6},{6,7},{7,8},{8,9},{9,10},{10,1... | collective-permute-start | bytes 1179656 | tf_op jit(solution)/shard_map/ppermute | solution.py:12
  321.2 70.5 %collective-permute-start.9 = (f32[384,256]{0,1:T(8,128)S(1)}, f32[384,256]{0,1:T(8,128)}, u32[]{:S(2)}, u32[]{:S(2)}) collective-permute-start(f32[384,256]{0,1:T(8,128)S(1)} %get-tuple-element.23), channel_id=1, source_target_pairs={{16,0},{32,16},{48,32},{64,48},{80,64},{96,80},{112,96},{17,1},{33... | collective-permute-start | bytes 1179656 | tf_op jit(solution)/shard_map/ppermute | solution.py:12
  323.7 68.0 %collective-permute-start.8 = (f32[384,256]{0,1:T(8,128)S(1)}, f32[384,256]{0,1:T(8,128)}, u32[]{:S(2)}, u32[]{:S(2)}) collective-permute-start(f32[384,256]{0,1:T(8,128)S(1)} %get-tuple-element.20), channel_id=1, source_target_pairs={{0,16},{16,32},{32,48},{48,64},{64,80},{80,96},{96,112},{1,17},{17... | collective-permute-start | bytes 1179656 | tf_op jit(solution)/shard_map/ppermute | solution.py:12
  413.9 3.1 copy-start.4
  419.9 7.6 copy-start.10
  427.5 1.4 copy-start.11
  428.9 76.0 %collective-permute-start.15 = (f32[384,256]{0,1:T(8,128)}, f32[384,256]{0,1:T(8,128)S(1)}, u32[]{:S(2)}, u32[]{:S(2)}) collective-permute-start(f32[384,256]{0,1:T(8,128)} %get-tuple-element.15), channel_id=1, source_target_pairs={{1,0},{2,1},{3,2},{4,3},{5,4},{6,5},{7,6},{8,7},{9,8},{10,9},{11,1... | collective-permute-start | bytes 1179656 | tf_op jit(solution)/shard_map/ppermute | solution.py:12
  430.2 74.7 %collective-permute-start.14 = (f32[384,256]{0,1:T(8,128)}, f32[384,256]{0,1:T(8,128)S(1)}, u32[]{:S(2)}, u32[]{:S(2)}) collective-permute-start(f32[384,256]{0,1:T(8,128)} %get-tuple-element.16), channel_id=1, source_target_pairs={{0,1},{1,2},{2,3},{3,4},{4,5},{5,6},{6,7},{7,8},{8,9},{9,10},{10,1... | collective-permute-start | bytes 1179656 | tf_op jit(solution)/shard_map/ppermute | solution.py:12
  434.2 70.7 %collective-permute-start.13 = (f32[384,256]{0,1:T(8,128)S(1)}, f32[384,256]{0,1:T(8,128)}, u32[]{:S(2)}, u32[]{:S(2)}) collective-permute-start(f32[384,256]{0,1:T(8,128)S(1)} %get-tuple-element.17), channel_id=1, source_target_pairs={{16,0},{32,16},{48,32},{64,48},{80,64},{96,80},{112,96},{17,1},{33... | collective-permute-start | bytes 1179656 | tf_op jit(solution)/shard_map/ppermute | solution.py:12
  437.6 67.3 %collective-permute-start.12 = (f32[384,256]{0,1:T(8,128)S(1)}, f32[384,256]{0,1:T(8,128)}, u32[]{:S(2)}, u32[]{:S(2)}) collective-permute-start(f32[384,256]{0,1:T(8,128)S(1)} %get-tuple-element.14), channel_id=1, source_target_pairs={{0,16},{16,32},{32,48},{48,64},{64,80},{80,96},{96,112},{1,17},{17... | collective-permute-start | bytes 1179656 | tf_op jit(solution)/shard_map/ppermute | solution.py:12
  532.4 205.1 %copy-start.1 = (f32[1536,256]{0,1:T(8,128)}, f32[1536,256]{0,1:T(8,128)S(1)}, u32[]{:S(2)}) copy-start(f32[1536,256]{0,1:T(8,128)S(1)} %multiply_add_fusion) | copy-start | bytes 4718596
  740.0 1.4 copy-start.9
  741.4 76.0 %collective-permute-start.19 = (f32[384,256]{0,1:T(8,128)}, f32[384,256]{0,1:T(8,128)S(1)}, u32[]{:S(2)}, u32[]{:S(2)}) collective-permute-start(f32[384,256]{0,1:T(8,128)} %get-tuple-element.11), channel_id=1, source_target_pairs={{1,0},{2,1},{3,2},{4,3},{5,4},{6,5},{7,6},{8,7},{9,8},{10,9},{11,1... | collective-permute-start | bytes 1179656 | tf_op jit(solution)/shard_map/ppermute | solution.py:12
  742.7 74.8 %collective-permute-start.18 = (f32[384,256]{0,1:T(8,128)}, f32[384,256]{0,1:T(8,128)S(1)}, u32[]{:S(2)}, u32[]{:S(2)}) collective-permute-start(f32[384,256]{0,1:T(8,128)} %get-tuple-element.12), channel_id=1, source_target_pairs={{0,1},{1,2},{2,3},{3,4},{4,5},{5,6},{6,7},{7,8},{8,9},{9,10},{10,1... | collective-permute-start | bytes 1179656 | tf_op jit(solution)/shard_map/ppermute | solution.py:12
  746.7 70.7 %collective-permute-start.17 = (f32[384,256]{0,1:T(8,128)S(1)}, f32[384,256]{0,1:T(8,128)}, u32[]{:S(2)}, u32[]{:S(2)}) collective-permute-start(f32[384,256]{0,1:T(8,128)S(1)} %get-tuple-element.13), channel_id=1, source_target_pairs={{16,0},{32,16},{48,32},{64,48},{80,64},{96,80},{112,96},{17,1},{33... | collective-permute-start | bytes 1179656 | tf_op jit(solution)/shard_map/ppermute | solution.py:12
  749.2 68.3 %collective-permute-start.16 = (f32[384,256]{0,1:T(8,128)S(1)}, f32[384,256]{0,1:T(8,128)}, u32[]{:S(2)}, u32[]{:S(2)}) collective-permute-start(f32[384,256]{0,1:T(8,128)S(1)} %get-tuple-element.10), channel_id=1, source_target_pairs={{0,16},{16,32},{32,48},{48,64},{64,80},{80,96},{96,112},{1,17},{17... | collective-permute-start | bytes 1179656 | tf_op jit(solution)/shard_map/ppermute | solution.py:12
  839.7 3.1 copy-start.2
  847.6 3.1 copy-start.12
Sparse Core Ops, SparseCore 0:
  100.5 151.7 all-reduce.5
  534.6 141.8 all-reduce.7

commit v2 on v1

v2 whole, which is shorter than its diff:
```python
import jax
import jax.numpy as jnp
from jax import lax
from jax.sharding import PartitionSpec as P

HIGH = lax.Precision.HIGH
HIGHEST = lax.Precision.HIGHEST


def shifted(block, axis, distance):
    devices = range(lax.axis_size(axis))
    route = [(i - distance, i) for i in devices if i - distance in devices]
    return lax.ppermute(block, axis, route)


def facing(faces):
    return (
        shifted(faces[1], "sx", 1),
        shifted(faces[0], "sx", -1),
        shifted(faces[3], "sy", 1),
        shifted(faces[2], "sy", -1),
    )


def jump(field, match):
    size = field.shape[0] // 4
    faces = [field[f * size : (f + 1) * size] for f in range(4)]
    received = facing(faces)
    return jnp.concatenate(
        [faces[f] - jnp.dot(match[f], received[f], precision=HIGHEST) for f in range(4)], axis=0
    )


def inner(first, second):
    return jnp.sum(first * second, axis=0)


def shards(loads, schur_flex, dirichlet, coupling, corner_index, face_lists, coarse_inverse):
    flex_mat = schur_flex[0, 0]
    prec_mat = dirichlet[0, 0]
    coupling_mat = coupling[0, 0]
    corners = corner_index[0, 0]
    face_index = face_lists[0, 0]
    ncoarse = coarse_inverse.shape[1]
    ncl = corners.shape[0]
    size = face_index.shape[1]
    sx = lax.axis_index("sx")
    sy = lax.axis_index("sy")
    inside = jnp.stack([sx > 0, sx < lax.axis_size("sx") - 1, sy > 0, sy < lax.axis_size("sy") - 1])
    scale = jnp.repeat(1.0 + inside.astype(jnp.float32), size)[:, None]
    match = (face_index[:, :, None] == jnp.arange(size, dtype=jnp.int32)[None, None, :]).astype(jnp.float32)
    inverse = lax.all_gather(coarse_inverse, ("sx", "sy"), axis=0, tiled=True)

    slots = jnp.concatenate([corners, jnp.arange(ncoarse + 1, ncoarse + 4, dtype=jnp.int32)])
    place = (slots[None, :] == jnp.arange(ncoarse + 8, dtype=jnp.int32)[:, None]).astype(jnp.float32)

    coarse_ids = jnp.arange(ncoarse, dtype=jnp.float32)[None, :]
    own = corners.astype(jnp.float32)
    parts = [coupling_mat[:, f * size : (f + 1) * size].T for f in range(4)]
    tagged = [jnp.concatenate([part, jnp.broadcast_to(own, (8, ncl))], axis=0) for part in parts]
    pick = (own[:, None] == coarse_ids).astype(jnp.float32)
    columns = []
    for f, got in enumerate(facing(tagged)):
        their_pick = (got[size][:, None] == coarse_ids).astype(jnp.float32)
        theirs = jnp.dot(match[f], got[:size], precision=HIGHEST)
        columns.append(
            jnp.dot(parts[f], pick, precision=HIGHEST) - jnp.dot(theirs, their_pick, precision=HIGHEST)
        )
    coupling_jump = jnp.concatenate(columns, axis=0)

    def reduced(local_load, *rows):
        rows = list(rows) + [jnp.zeros_like(rows[0])] * (3 - len(rows))
        block = jnp.concatenate([local_load] + [row[None] for row in rows], axis=0)
        total = lax.psum(jnp.dot(place, block, precision=HIGHEST), ("sx", "sy"))
        return total[:ncoarse], total[ncoarse + 1], total[ncoarse + 2], total[ncoarse + 3]

    def coarse(rhs):
        sol = jnp.dot(inverse, rhs, precision=HIGHEST)
        return jnp.dot(coupling_jump, sol, precision=HIGHEST), inner(rhs, sol)

    def precondition(residual):
        spread = scale * residual
        applied = jnp.dot(prec_mat, spread, precision=HIGH)
        return 0.5 * jump(applied, match), 0.5 * inner(spread, applied)

    def flexible(direction):
        spread = scale * direction
        return spread, jnp.dot(flex_mat, spread, precision=HIGH), jnp.dot(coupling_mat, spread, precision=HIGH)

    residual = jump(loads[0, 0], match)
    direction, dot_part = precondition(residual)
    spread, flexed, load = flexible(direction)
    rhs, res_dot, energy, _ = reduced(load, dot_part, inner(spread, flexed))
    image = jump(flexed, match)
    correction, coarse_energy = coarse(rhs)
    step = res_dot / (energy + coarse_energy)
    residual = residual - step * (image + correction)
    multipliers = step * direction

    precond, dot_part = precondition(residual)
    spread, new_flexed, load = flexible(precond)
    new_rhs, new_dot, new_energy, cross = reduced(
        load, dot_part, inner(spread, new_flexed), inner(spread, flexed)
    )
    new_image = jump(new_flexed, match)
    beta = new_dot / res_dot
    rhs = new_rhs + beta * rhs
    energy = new_energy + beta * (2.0 * cross + beta * energy)
    correction, coarse_energy = coarse(rhs)
    step = new_dot / (energy + coarse_energy)
    multipliers = multipliers + step * (precond + beta * direction)
    residual = residual - step * (new_image + beta * image + correction)
    return (multipliers[None, None], residual[None, None])


def solution(mesh):
    return jax.shard_map(
        shards,
        mesh=mesh,
        in_specs=(
            P("sx", "sy", None, None),
            P("sx", "sy", None, None),
            P("sx", "sy", None, None),
            P("sx", "sy", None, None),
            P("sx", "sy", None),
            P("sx", "sy", None, None),
            P(("sx", "sy"), None),
        ),
        out_specs=(P("sx", "sy", None, None), P("sx", "sy", None, None)),
        check_vma=False,
    )
```

time: 861 us -> 486 us (0.56)
  blocking collectives: 303 us -> 0 us
  local copies, waits for them, and re-layouts: 130 us -> 12.4 us
  matrix products: 44.1 us -> 78.2 us
  other arithmetic: 24 us -> 9.11 us
  waiting for transfers between devices: 285 us -> 297 us
  starting transfers between devices: 58.1 us -> 68.4 us
    psum x3 -> x0, blocking collectives: 195 us -> none  [total(): return lax.psum(values, ('sx', 'sy'))]
    all_gather x2 -> x0, blocking collectives: 108 us -> none  [coarse_solve(): return lax.all_gather(mine, ('sx', 'sy'), axis=0, tiled=True)]
    gather x12 -> x0, local copies, waits for them, and re-layouts: 99.6 us -> none  [the longest x10 96.4 us: jump(): matched = received[jnp.arange(4, dtype=jnp.int32)[:, None], face_index]]
    dot_general x12 -> x44, matrix products: 44.1 us -> 78.2 us  [the longest x20 23.1 us: jump(): jnp.dot(match[f], received[f], precision=HIGHEST)]
    ppermute x20 -> x24, waiting for transfers between devices: 5.83 us -> 23.2 us  [shifted(): return lax.ppermute(block, axis, route)]
    another operation x5 -> x0, other arithmetic: 11.2 us -> none  [jump(): jnp.stack([from_low_x, from_high_x, from_low_y, from_high_y], axis=0)]
    unnamed x41 -> x85, local copies, waits for them, and re-layouts: 12.9 us -> 1.78 us
    ppermute x20 -> x24, starting transfers between devices: 57.8 us -> 68.1 us  [shifted(): return lax.ppermute(block, axis, route)]
  transfers between devices with their start and end apart: 22 -> 27, of which waited for: 8 -> 9; matrix products, arithmetic and copies ran while one was open for 2% -> 13% of each run, Pallas kernels for 0% -> 0%
where the time goes in v2:
time: 486 us; the launch traced here: 480 us
  waiting for transfers between devices  297 us (61%)
  matrix products  78.2 us (16%)
  starting transfers between devices  68.4 us (14%)
  between operations  15.1 us (3%)
  local copies, waits for them, and re-layouts  12.4 us (3%)
  other arithmetic  9.11 us (2%)
    psum x2, waiting for transfers between devices, reduced(): total = lax.psum(jnp.dot(place, block, precision=HIGHEST), ('sx', 'sy'))  273 us
    ppermute x24, starting transfers between devices, shifted(): return lax.ppermute(block, axis, route)  68.1 us
    ppermute x24, waiting for transfers between devices, shifted(): return lax.ppermute(block, axis, route)  23.2 us
    dot_general x20, matrix products, jump(): jnp.dot(match[f], received[f], precision=HIGHEST)  23.1 us
    dot_general x2, matrix products, precondition(): applied = jnp.dot(prec_mat, spread, precision=HIGH)  11.6 us
    dot_general x2, matrix products, coarse(): return (jnp.dot(coupling_jump, sol, precision=HIGHEST), inner(rhs, sol))  10.9 us
    dot_general x2, matrix products, flexible(): jnp.dot(flex_mat, spread, precision=HIGH)  9.93 us
  transfers between devices with their start and end apart: 27, of which 9 were waited for; matrix products, arithmetic and copies ran while one was open for 13% of the time, Pallas kernels for 0%

profile of v2, /device:TPU:1, one launch (start us, length us, event | category | flops | bytes accessed | tf_op | source)
XLA Modules:
  0.0 480.3 jit_solution(9736556489605518894)
XLA Ops:
  9.5 4.6 collective-permute-start.12
  14.1 1.9 collective-permute-start.13
  16.0 3.5 collective-permute-start.14
  19.6 1.4 collective-permute-start.15
  21.0 2.5 slice_bitcast_fusion.6
  23.5 3.9 collective-permute-start
  27.5 1.4 convolution_bitcast_fusion
  31.2 1.9 collective-permute-start.1
  33.7 2.7 convolution_subtract_fusion
  36.4 4.3 collective-permute-start.2
  41.2 1.4 convolution_subtract_fusion.1
  42.6 1.9 collective-permute-start.3
  45.0 1.4 convolution_subtract_fusion.2
  47.0 1.6 convolution_subtract_fusion.23
  49.7 5.8 %collective-permute-done.3 = f32[384,256]{1,0:T(8,128)S(1)} collective-permute-done((f32[384,256]{1,0:T(8,128)S(1)}, f32[384,256]{1,0:T(8,128)S(1)}, u32[]{:S(2)}, u32[]{:S(2)}) %collective-permute-start.3) | collective-permute-done | bytes 393248 | tf_op jit(solution)/shard_map/ppermute | solution.py:13
  56.1 4.1 multiply_reduce_fusion.4
  60.4 4.6 collective-permute-start.4
  65.0 1.4 convolution_subtract_fusion.3
  66.4 3.4 collective-permute-start.6
  69.8 1.3 collective-permute-start.7
  71.1 2.5 collective-permute-start.5
  74.2 4.1 collective-permute-done.6
  78.8 3.3 collective-permute-done.7
  83.3 4.2 multiply_reduce_fusion.3
  88.4 4.1 collective-permute-start.8
  92.5 5.6 %collective-permute-start.10 = (f32[384,256]{1,0:T(8,128)}, f32[384,256]{1,0:T(8,128)}, u32[]{:S(2)}, u32[]{:S(2)}) collective-permute-start(f32[384,256]{1,0:T(8,128)} %get-tuple-element.13), channel_id=1, source_target_pairs={{0,1},{1,2},{2,3},{3,4},{4,5},{5,6},{6,7},{7,8},{8,9},{9,10},{10,1... | collective-permute-start | bytes 1179656 | tf_op jit(solution)/shard_map/ppermute | solution.py:13
  98.1 1.3 collective-permute-start.11
  99.4 1.9 collective-permute-start.9
  102.0 1.2 fusion.39
  103.5 2.3 convolution_subtract_fusion.15
  106.0 2.3 convolution_subtract_fusion.13
  108.3 2.3 collective-permute-done.11
  110.7 2.3 convolution_subtract_fusion.12
  113.0 2.3 convolution_subtract_fusion.14
  115.3 1.6 reshape.275
  116.8 134.1 %all-reduce.3.cloned.1.call-done = f32[520,256]{1,0:T(8,128)} async-done(((f32[520,256]{1,0:T(8,128)}), f32[520,256]{1,0:T(8,128)}) %all-reduce.3.cloned.1.call-update) | async-done | bytes 532496 | tf_op jit(solution)/shard_map/psum | solution.py:74
  251.0 3.7 fusion.36
  254.7 2.0 copy.28
  256.7 1.3 fusion.35
  258.8 5.7 %fusion.9 = f32[1536,256]{1,0:T(8,128)S(1)} fusion(f32[256,512]{1,0:T(8,128)} %fusion.36, f32[384,512]{1,0:T(8,128)} %convolution_subtract_fusion, f32[384,512]{1,0:T(8,128)} %convolution_subtract_fusion.1, f32[384,512]{1,0:T(8,128)} %convolution_subtract_fusion.2, f32[384,512]{1,0:T(8,128)} %convolution_subtract_fusion.3, ...), kind=kOutput, calls=%fused_computation.11 | convolution fusion | flops 2421817344 | bytes 8389632 | tf_op jit(solution)/shard_map/dot_general | solution.py:79
  264.6 7.4 %multiply_reduce_fusion.2 = (f32[256]{0:T(256)S(1)}, f32[1536,256]{1,0:T(8,128)S(1)}) fusion(f32[1536,256]{1,0:T(8,128)S(1)} %fusion.9, f32[1536]{0:T(1024)S(1)} %mul.194, f32[1,1,1536,1536]{3,2,1,0:T(8,128)} %param.9), kind=kOutput, calls=%fused_computation.34 | convolution fusion | flops 3625451264 | bytes 12590080 | tf_op jit(solution)/shard_map/dot_general | solution.py:83
  272.2 3.2 collective-permute-start.16
  275.3 1.9 collective-permute-start.18
  277.3 1.3 collective-permute-start.19
  278.6 2.5 collective-permute-start.17
  281.6 4.1 collective-permute-done.18
  286.2 3.3 collective-permute-done.19
  290.7 5.8 %multiply_reduce_fusion.1 = (f32[256]{0:T(256)S(1)}, f32[256]{0:T(256)S(1)}, f32[1536,256]{1,0:T(8,128)}) fusion(f32[1536]{0:T(1024)S(1)} %broadcast_multiply_fusion, f32[384,256]{1,0:T(8,128)S(1)} %convolution_subtract_fusion.8, f32[384,256]{1,0:T(8,128)S(1)} %convolution_subtract_fusion.9, f32[384,256]{1,0:T(8,128)S(1)} %convolution_subtract_fusion.10, ...), kind=kOutput, calls=%fused_computation.33 | convolution fusion | flops 3628596736 | bytes 14163968 | tf_op jit(solution)/shard_map/dot_general | solution.py:88
  297.1 1.2 fusion.38
  298.3 1.2 fusion.89
  299.5 3.8 collective-permute-start.20
  303.3 3.9 collective-permute-start.22
  307.2 1.3 collective-permute-start.23
  308.4 2.2 collective-permute-start.21
  310.6 139.0 %all-reduce.5.cloned.1.call-done = f32[520,256]{1,0:T(8,128)} async-done(((f32[520,256]{1,0:T(8,128)}), f32[520,256]{1,0:T(8,128)}) %all-reduce.5.cloned.1.call-update) | async-done | bytes 532496 | tf_op jit(solution)/shard_map/psum | solution.py:74
  450.4 3.9 fusion.40
  454.2 2.1 copy.31
  456.4 1.6 fusion.34
  458.9 2.7 fusion.25
  461.6 1.7 convolution_subtract_fusion.7
  463.3 1.7 convolution_subtract_fusion.5
  465.0 1.7 convolution_subtract_fusion.4
  466.7 1.5 convolution_subtract_fusion.6
  468.3 5.2 %fusion.29 = f32[1,1,1536,256]{3,2,1,0:T(8,128)} fusion(f32[1536,256]{1,0:T(8,128)S(1)} %copy-done.23, f32[384,256]{1,0:T(8,128)S(1)} %convolution_subtract_fusion.4, f32[384,256]{1,0:T(8,128)S(1)} %convolution_subtract_fusion.5, f32[384,256]{1,0:T(8,128)S(1)} %convolution_subtract_fusion.6, f32[384,256]{1,0:T(8,128)S(1)} %convolution_subtract_fusion.7, ...), kind=kOutput, calls=%fused_computation.31 | convolution fusion | flops 2422603776 | bytes 9963520 | tf_op jit(solution)/shard_map/dot_general | solution.py:79
  (157 shorter events, 18.0 us)
Async XLA Ops:
  7.2 108.1 %all-gather.3.cloned.1.call-start = ((), (), s32[]{:S(2)}) async-start(), calls=%async_computation.2 | async-start | bytes 1056768 | tf_op jit(solution)/shard_map/all_gather | solution.py:52
  7.9 243.1 %all-reduce.3.cloned.1.call-start = ((), (), s32[]{:S(2)}) async-start(), calls=%async_computation | async-start | bytes 1064960 | tf_op jit(solution)/shard_map/psum | solution.py:74
  9.5 36.9 %collective-permute-start.12 = (f32[392,16]{0,1:T(8,128)S(1)}, f32[392,16]{0,1:T(8,128)S(1)}, u32[]{:S(2)}, u32[]{:S(2)}) collective-permute-start(f32[392,16]{0,1:T(8,128)S(1)} %get-tuple-element.28), channel_id=1, source_target_pairs={{0,16},{16,32},{32,48},{48,64},{64,80},{80,96},{96,112},{1,17},{17... | collective-permute-start | bytes 75272 | tf_op jit(solution)/shard_map/ppermute | solution.py:13
  14.1 28.5 %collective-permute-start.13 = (f32[392,16]{0,1:T(8,128)S(1)}, f32[392,16]{0,1:T(8,128)S(1)}, u32[]{:S(2)}, u32[]{:S(2)}) collective-permute-start(f32[392,16]{0,1:T(8,128)S(1)} %get-tuple-element.29), channel_id=1, source_target_pairs={{16,0},{32,16},{48,32},{64,48},{80,64},{96,80},{112,96},{17,1},{33... | collective-permute-start | bytes 75272 | tf_op jit(solution)/shard_map/ppermute | solution.py:13
  16.0 20.4 %collective-permute-start.14 = (f32[392,16]{0,1:T(8,128)S(1)}, f32[392,16]{0,1:T(8,128)S(1)}, u32[]{:S(2)}, u32[]{:S(2)}) collective-permute-start(f32[392,16]{0,1:T(8,128)S(1)} %get-tuple-element.30), channel_id=1, source_target_pairs={{0,1},{1,2},{2,3},{3,4},{4,5},{5,6},{6,7},{7,8},{8,9},{9,10},{10,1... | collective-permute-start | bytes 75272 | tf_op jit(solution)/shard_map/ppermute | solution.py:13
  19.6 7.9 %copy-start.28 = (f32[1,1,16,1536]{3,2,1,0:T(8,128)S(1)}, f32[1,1,16,1536]{3,2,1,0:T(8,128)}, u32[]{:S(2)}) copy-start(f32[1,1,16,1536]{3,2,1,0:T(8,128)} %param.10) | copy-start | bytes 294916
  19.6 11.7 %collective-permute-start.15 = (f32[392,16]{0,1:T(8,128)S(1)}, f32[392,16]{0,1:T(8,128)S(1)}, u32[]{:S(2)}, u32[]{:S(2)}) collective-permute-start(f32[392,16]{0,1:T(8,128)S(1)} %get-tuple-element.31), channel_id=1, source_target_pairs={{1,0},{2,1},{3,2},{4,3},{5,4},{6,5},{7,6},{8,7},{9,8},{10,9},{11,1... | collective-permute-start | bytes 75272 | tf_op jit(solution)/shard_map/ppermute | solution.py:13
  23.5 23.4 %collective-permute-start = (f32[384,256]{1,0:T(8,128)}, f32[384,256]{1,0:T(8,128)}, u32[]{:S(2)}, u32[]{:S(2)}) collective-permute-start(f32[384,256]{1,0:T(8,128)} %get-tuple-element.20), channel_id=1, source_target_pairs={{0,16},{16,32},{32,48},{48,64},{64,80},{80,96},{96,112},{1,17},{17... | collective-permute-start | bytes 1179656 | tf_op jit(solution)/shard_map/ppermute | solution.py:13
  27.5 3.2 copy-start.34
  31.2 17.3 %collective-permute-start.1 = (f32[384,256]{1,0:T(8,128)}, f32[384,256]{1,0:T(8,128)S(1)}, u32[]{:S(2)}, u32[]{:S(2)}) collective-permute-start(f32[384,256]{1,0:T(8,128)} %get-tuple-element.21), channel_id=1, source_target_pairs={{16,0},{32,16},{48,32},{64,48},{80,64},{96,80},{112,96},{17,1},{33... | collective-permute-start | bytes 1179656 | tf_op jit(solution)/shard_map/ppermute | solution.py:13
  33.7 8.9 %copy-start.29 = (f32[384,256]{1,0:T(8,128)S(1)}, f32[384,256]{1,0:T(8,128)}, u32[]{:S(2)}) copy-start(f32[384,256]{1,0:T(8,128)} %get-tuple-element.23) | copy-start | bytes 1179652
  33.7 13.3 %copy-start.10 = (f32[1,1,1536,256]{3,2,1,0:T(8,128)S(1)}, f32[1,1,1536,256]{3,2,1,0:T(8,128)}, u32[]{:S(2)}) copy-start(f32[1,1,1536,256]{3,2,1,0:T(8,128)} %param.7) | copy-start | bytes 4718596
  36.4 12.7 %collective-permute-start.2 = (f32[384,256]{1,0:T(8,128)}, f32[384,256]{1,0:T(8,128)S(1)}, u32[]{:S(2)}, u32[]{:S(2)}) collective-permute-start(f32[384,256]{1,0:T(8,128)} %get-tuple-element.22), channel_id=1, source_target_pairs={{0,1},{1,2},{2,3},{3,4},{4,5},{5,6},{6,7},{7,8},{8,9},{9,10},{10,1... | collective-permute-start | bytes 1179656 | tf_op jit(solution)/shard_map/ppermute | solution.py:13
  40.8 15.3 %copy-start = (f32[1,1,1536,1536]{3,2,1,0:T(8,128)S(1)}, f32[1,1,1536,1536]{3,2,1,0:T(8,128)}, u32[]{:S(2)}) copy-start(f32[1,1,1536,1536]{3,2,1,0:T(8,128)} %param.9) | copy-start | bytes 28311556
  42.6 12.9 %collective-permute-start.3 = (f32[384,256]{1,0:T(8,128)S(1)}, f32[384,256]{1,0:T(8,128)S(1)}, u32[]{:S(2)}, u32[]{:S(2)}) collective-permute-start(f32[384,256]{1,0:T(8,128)S(1)} %copy-done.29), channel_id=1, source_target_pairs={{1,0},{2,1},{3,2},{4,3},{5,4},{6,5},{7,6},{8,7},{9,8},{10,9},{11,1... | collective-permute-start | bytes 1179656 | tf_op jit(solution)/shard_map/ppermute | solution.py:13
  48.5 7.5 %copy-start.17 = (f32[384,256]{1,0:T(8,128)}, f32[384,256]{1,0:T(8,128)S(1)}, u32[]{:S(2)}) copy-start(f32[384,256]{1,0:T(8,128)S(1)} %convolution_subtract_fusion.23) | copy-start | bytes 1179652
  49.1 11.1 %copy-start.18 = (f32[384,256]{1,0:T(8,128)}, f32[384,256]{1,0:T(8,128)S(1)}, u32[]{:S(2)}) copy-start(f32[384,256]{1,0:T(8,128)S(1)} %convolution_subtract_fusion.22) | copy-start | bytes 1179652
  49.7 10.6 %copy-start.19 = (f32[384,256]{1,0:T(8,128)}, f32[384,256]{1,0:T(8,128)S(1)}, u32[]{:S(2)}) copy-start(f32[384,256]{1,0:T(8,128)S(1)} %convolution_subtract_fusion.21) | copy-start | bytes 1179652
  56.0 4.2 copy-start.20
  56.1 27.2 %slice-start = ((s8[9437184]{0:T(1024)(128)(4,1)}), s8[4194304]{0:T(1024)(128)(4,1)S(1)}, s32[]{:S(2)}) async-start(s8[9437184]{0:T(1024)(128)(4,1)} %bitcast.172), calls=%async_computation.3 | async-start | bytes 8388608
  56.1 27.2 %slice-start.1 = ((s8[9437184]{0:T(1024)(128)(4,1)}), s8[1048576]{0:T(1024)(128)(4,1)S(1)}, s32[]{:S(2)}) async-start(s8[9437184]{0:T(1024)(128)(4,1)} %bitcast.172), calls=%async_computation.4 | async-start | bytes 2097152
  60.3 23.0 %slice-start.2 = ((s8[9437184]{0:T(1024)(128)(4,1)}), s8[4194304]{0:T(1024)(128)(4,1)S(1)}, s32[]{:S(2)}) async-start(s8[9437184]{0:T(1024)(128)(4,1)} %bitcast.172), calls=%async_computation.5 | async-start | bytes 8388608
  60.4 13.2 %collective-permute-start.4 = (f32[384,256]{1,0:T(8,128)S(1)}, f32[384,256]{1,0:T(8,128)S(1)}, u32[]{:S(2)}, u32[]{:S(2)}) collective-permute-start(f32[384,256]{1,0:T(8,128)S(1)} %get-tuple-element.16), channel_id=1, source_target_pairs={{0,16},{16,32},{32,48},{48,64},{64,80},{80,96},{96,112},{1,17},{17... | collective-permute-start | bytes 1179656 | tf_op jit(solution)/shard_map/ppermute | solution.py:13
  66.4 11.9 %collective-permute-start.6 = (f32[384,256]{1,0:T(8,128)S(1)}, f32[384,256]{1,0:T(8,128)S(1)}, u32[]{:S(2)}, u32[]{:S(2)}) collective-permute-start(f32[384,256]{1,0:T(8,128)S(1)} %get-tuple-element.17), channel_id=1, source_target_pairs={{0,1},{1,2},{2,3},{3,4},{4,5},{5,6},{6,7},{7,8},{8,9},{9,10},{10,1... | collective-permute-start | bytes 1179656 | tf_op jit(solution)/shard_map/ppermute | solution.py:13
  69.8 12.4 %collective-permute-start.7 = (f32[384,256]{1,0:T(8,128)S(1)}, f32[384,256]{1,0:T(8,128)S(1)}, u32[]{:S(2)}, u32[]{:S(2)}) collective-permute-start(f32[384,256]{1,0:T(8,128)S(1)} %get-tuple-element.18), channel_id=1, source_target_pairs={{1,0},{2,1},{3,2},{4,3},{5,4},{6,5},{7,6},{8,7},{9,8},{10,9},{11,1... | collective-permute-start | bytes 1179656 | tf_op jit(solution)/shard_map/ppermute | solution.py:13
  71.1 11.6 %collective-permute-start.5 = (f32[384,256]{1,0:T(8,128)S(1)}, f32[384,256]{1,0:T(8,128)S(1)}, u32[]{:S(2)}, u32[]{:S(2)}) collective-permute-start(f32[384,256]{1,0:T(8,128)S(1)} %get-tuple-element.19), channel_id=1, source_target_pairs={{16,0},{32,16},{48,32},{64,48},{80,64},{96,80},{112,96},{17,1},{33... | collective-permute-start | bytes 1179656 | tf_op jit(solution)/shard_map/ppermute | solution.py:13
  74.1 27.2 %copy-start.2 = (f32[384,256]{1,0:T(8,128)}, f32[384,256]{1,0:T(8,128)S(1)}, u32[]{:S(2)}) copy-start(f32[384,256]{1,0:T(8,128)S(1)} %convolution_subtract_fusion.19) | copy-start | bytes 1179652
  78.8 22.5 %copy-start.4 = (f32[384,256]{1,0:T(8,128)}, f32[384,256]{1,0:T(8,128)S(1)}, u32[]{:S(2)}) copy-start(f32[384,256]{1,0:T(8,128)S(1)} %convolution_subtract_fusion.17) | copy-start | bytes 1179652
  82.7 18.7 %copy-start.6 = (f32[384,256]{1,0:T(8,128)}, f32[384,256]{1,0:T(8,128)S(1)}, u32[]{:S(2)}) copy-start(f32[384,256]{1,0:T(8,128)S(1)} %convolution_subtract_fusion.16) | copy-start | bytes 1179652
  83.3 18.1 %copy-start.8 = (f32[384,256]{1,0:T(8,128)}, f32[384,256]{1,0:T(8,128)S(1)}, u32[]{:S(2)}) copy-start(f32[384,256]{1,0:T(8,128)S(1)} %convolution_subtract_fusion.18) | copy-start | bytes 1179652
  88.4 15.0 %collective-permute-start.8 = (f32[384,256]{1,0:T(8,128)}, f32[384,256]{1,0:T(8,128)}, u32[]{:S(2)}, u32[]{:S(2)}) collective-permute-start(f32[384,256]{1,0:T(8,128)} %get-tuple-element.12), channel_id=1, source_target_pairs={{0,16},{16,32},{32,48},{48,64},{64,80},{80,96},{96,112},{1,17},{17... | collective-permute-start | bytes 1179656 | tf_op jit(solution)/shard_map/ppermute | solution.py:13
  92.5 13.6 %collective-permute-start.10 = (f32[384,256]{1,0:T(8,128)}, f32[384,256]{1,0:T(8,128)}, u32[]{:S(2)}, u32[]{:S(2)}) collective-permute-start(f32[384,256]{1,0:T(8,128)} %get-tuple-element.13), channel_id=1, source_target_pairs={{0,1},{1,2},{2,3},{3,4},{4,5},{5,6},{6,7},{7,8},{8,9},{9,10},{10,1... | collective-permute-start | bytes 1179656 | tf_op jit(solution)/shard_map/ppermute | solution.py:13
  98.1 12.5 %collective-permute-start.11 = (f32[384,256]{1,0:T(8,128)S(1)}, f32[384,256]{1,0:T(8,128)}, u32[]{:S(2)}, u32[]{:S(2)}) collective-permute-start(f32[384,256]{1,0:T(8,128)S(1)} %get-tuple-element.14), channel_id=1, source_target_pairs={{1,0},{2,1},{3,2},{4,3},{5,4},{6,5},{7,6},{8,7},{9,8},{10,9},{11,1... | collective-permute-start | bytes 1179656 | tf_op jit(solution)/shard_map/ppermute | solution.py:13
  99.4 13.6 %collective-permute-start.9 = (f32[384,256]{1,0:T(8,128)S(1)}, f32[384,256]{1,0:T(8,128)}, u32[]{:S(2)}, u32[]{:S(2)}) collective-permute-start(f32[384,256]{1,0:T(8,128)S(1)} %get-tuple-element.15), channel_id=1, source_target_pairs={{16,0},{32,16},{48,32},{64,48},{80,64},{96,80},{112,96},{17,1},{33... | collective-permute-start | bytes 1179656 | tf_op jit(solution)/shard_map/ppermute | solution.py:13
  103.2 346.4 %all-reduce.5.cloned.1.call-start = ((), (), s32[]{:S(2)}) async-start(), calls=%async_computation.1 | async-start | bytes 1064960 | tf_op jit(solution)/shard_map/psum | solution.py:74
  264.5 7.5 %copy-start.22 = (f32[1536,256]{1,0:T(8,128)}, f32[1536,256]{1,0:T(8,128)S(1)}, u32[]{:S(2)}) copy-start(f32[1536,256]{1,0:T(8,128)S(1)} %fusion.9) | copy-start | bytes 4718596
  264.5 26.1 %slice-start.3 = ((s8[9437184]{0:T(1024)(128)(4,1)}), s8[4194304]{0:T(1024)(128)(4,1)S(1)}, s32[]{:S(2)}) async-start(s8[9437184]{0:T(1024)(128)(4,1)} %bitcast.174), calls=%async_computation.6 | async-start | bytes 8388608
  264.6 26.1 %slice-start.4 = ((s8[9437184]{0:T(1024)(128)(4,1)}), s8[4194304]{0:T(1024)(128)(4,1)S(1)}, s32[]{:S(2)}) async-start(s8[9437184]{0:T(1024)(128)(4,1)} %bitcast.174), calls=%async_computation.7 | async-start | bytes 8388608
  272.0 18.6 %slice-start.5 = ((s8[9437184]{0:T(1024)(128)(4,1)}), s8[1048576]{0:T(1024)(128)(4,1)S(1)}, s32[]{:S(2)}) async-start(s8[9437184]{0:T(1024)(128)(4,1)} %bitcast.174), calls=%async_computation.8 | async-start | bytes 2097152
  272.2 8.9 %collective-permute-start.16 = (f32[384,256]{1,0:T(8,128)S(1)}, f32[384,256]{1,0:T(8,128)S(1)}, u32[]{:S(2)}, u32[]{:S(2)}) collective-permute-start(f32[384,256]{1,0:T(8,128)S(1)} %get-tuple-element.8), channel_id=1, source_target_pairs={{0,16},{16,32},{32,48},{48,64},{64,80},{80,96},{96,112},{1,17},{17... | collective-permute-start | bytes 1179656 | tf_op jit(solution)/shard_map/ppermute | solution.py:13
  275.3 10.4 %collective-permute-start.18 = (f32[384,256]{1,0:T(8,128)S(1)}, f32[384,256]{1,0:T(8,128)S(1)}, u32[]{:S(2)}, u32[]{:S(2)}) collective-permute-start(f32[384,256]{1,0:T(8,128)S(1)} %get-tuple-element.9), channel_id=1, source_target_pairs={{0,1},{1,2},{2,3},{3,4},{4,5},{5,6},{6,7},{7,8},{8,9},{9,10},{10,1... | collective-permute-start | bytes 1179656 | tf_op jit(solution)/shard_map/ppermute | solution.py:13
  277.3 12.2 %collective-permute-start.19 = (f32[384,256]{1,0:T(8,128)S(1)}, f32[384,256]{1,0:T(8,128)S(1)}, u32[]{:S(2)}, u32[]{:S(2)}) collective-permute-start(f32[384,256]{1,0:T(8,128)S(1)} %get-tuple-element.10), channel_id=1, source_target_pairs={{1,0},{2,1},{3,2},{4,3},{5,4},{6,5},{7,6},{8,7},{9,8},{10,9},{11,1... | collective-permute-start | bytes 1179656 | tf_op jit(solution)/shard_map/ppermute | solution.py:13
  278.6 11.5 %collective-permute-start.17 = (f32[384,256]{1,0:T(8,128)S(1)}, f32[384,256]{1,0:T(8,128)S(1)}, u32[]{:S(2)}, u32[]{:S(2)}) collective-permute-start(f32[384,256]{1,0:T(8,128)S(1)} %get-tuple-element.11), channel_id=1, source_target_pairs={{16,0},{32,16},{48,32},{64,48},{80,64},{96,80},{112,96},{17,1},{33... | collective-permute-start | bytes 1179656 | tf_op jit(solution)/shard_map/ppermute | solution.py:13
  281.6 14.8 %copy-start.11 = (f32[384,256]{1,0:T(8,128)}, f32[384,256]{1,0:T(8,128)S(1)}, u32[]{:S(2)}) copy-start(f32[384,256]{1,0:T(8,128)S(1)} %convolution_subtract_fusion.11) | copy-start | bytes 1179652
  286.2 10.2 %copy-start.13 = (f32[384,256]{1,0:T(8,128)}, f32[384,256]{1,0:T(8,128)S(1)}, u32[]{:S(2)}) copy-start(f32[384,256]{1,0:T(8,128)S(1)} %convolution_subtract_fusion.9) | copy-start | bytes 1179652
  290.1 6.4 %copy-start.15 = (f32[384,256]{1,0:T(8,128)}, f32[384,256]{1,0:T(8,128)S(1)}, u32[]{:S(2)}) copy-start(f32[384,256]{1,0:T(8,128)S(1)} %convolution_subtract_fusion.8) | copy-start | bytes 1179652
  290.7 5.8 %copy-start.16 = (f32[384,256]{1,0:T(8,128)}, f32[384,256]{1,0:T(8,128)S(1)}, u32[]{:S(2)}) copy-start(f32[384,256]{1,0:T(8,128)S(1)} %convolution_subtract_fusion.10) | copy-start | bytes 1179652
  299.5 162.1 %collective-permute-start.20 = (f32[384,256]{1,0:T(8,128)}, f32[384,256]{1,0:T(8,128)}, u32[]{:S(2)}, u32[]{:S(2)}) collective-permute-start(f32[384,256]{1,0:T(8,128)} %get-tuple-element.4), channel_id=1, source_target_pairs={{0,16},{16,32},{32,48},{48,64},{64,80},{80,96},{96,112},{1,17},{17... | collective-permute-start | bytes 1179656 | tf_op jit(solution)/shard_map/ppermute | solution.py:13
  303.3 160.0 %collective-permute-start.22 = (f32[384,256]{1,0:T(8,128)}, f32[384,256]{1,0:T(8,128)}, u32[]{:S(2)}, u32[]{:S(2)}) collective-permute-start(f32[384,256]{1,0:T(8,128)} %get-tuple-element.5), channel_id=1, source_target_pairs={{0,1},{1,2},{2,3},{3,4},{4,5},{5,6},{6,7},{7,8},{8,9},{9,10},{10,1... | collective-permute-start | bytes 1179656 | tf_op jit(solution)/shard_map/ppermute | solution.py:13
  307.2 157.8 %collective-permute-start.23 = (f32[384,256]{1,0:T(8,128)}, f32[384,256]{1,0:T(8,128)}, u32[]{:S(2)}, u32[]{:S(2)}) collective-permute-start(f32[384,256]{1,0:T(8,128)} %get-tuple-element.6), channel_id=1, source_target_pairs={{1,0},{2,1},{3,2},{4,3},{5,4},{6,5},{7,6},{8,7},{9,8},{10,9},{11,1... | collective-permute-start | bytes 1179656 | tf_op jit(solution)/shard_map/ppermute | solution.py:13
  308.4 158.2 %collective-permute-start.21 = (f32[384,256]{1,0:T(8,128)}, f32[384,256]{1,0:T(8,128)}, u32[]{:S(2)}, u32[]{:S(2)}) collective-permute-start(f32[384,256]{1,0:T(8,128)} %get-tuple-element.7), channel_id=1, source_target_pairs={{16,0},{32,16},{48,32},{64,48},{80,64},{96,80},{112,96},{17,1},{33... | collective-permute-start | bytes 1179656 | tf_op jit(solution)/shard_map/ppermute | solution.py:13
  454.2 4.5 copy-start.3
  454.2 4.5 copy-start.5
  454.2 4.6 copy-start.7
  458.8 9.4 %copy-start.30 = (f32[384,256]{1,0:T(8,128)S(1)}, f32[384,256]{1,0:T(8,128)}, u32[]{:S(2)}) copy-start(f32[384,256]{1,0:T(8,128)} %convolution_subtract_fusion.15) | copy-start | bytes 1179652
  458.8 9.4 %copy-start.31 = (f32[384,256]{1,0:T(8,128)S(1)}, f32[384,256]{1,0:T(8,128)}, u32[]{:S(2)}) copy-start(f32[384,256]{1,0:T(8,128)} %convolution_subtract_fusion.13) | copy-start | bytes 1179652
  458.9 9.4 %copy-start.32 = (f32[384,256]{1,0:T(8,128)S(1)}, f32[384,256]{1,0:T(8,128)}, u32[]{:S(2)}) copy-start(f32[384,256]{1,0:T(8,128)} %convolution_subtract_fusion.12) | copy-start | bytes 1179652
  458.9 9.4 %copy-start.33 = (f32[384,256]{1,0:T(8,128)S(1)}, f32[384,256]{1,0:T(8,128)}, u32[]{:S(2)}) copy-start(f32[384,256]{1,0:T(8,128)} %convolution_subtract_fusion.14) | copy-start | bytes 1179652
  461.6 6.7 %copy-start.26 = (f32[384,512]{1,0:T(8,128)S(1)}, f32[384,512]{1,0:T(8,128)}, u32[]{:S(2)}) copy-start(f32[384,512]{1,0:T(8,128)} %convolution_subtract_fusion.2) | copy-start | bytes 2359300
  461.6 6.7 %copy-start.27 = (f32[384,512]{1,0:T(8,128)S(1)}, f32[384,512]{1,0:T(8,128)}, u32[]{:S(2)}) copy-start(f32[384,512]{1,0:T(8,128)} %convolution_subtract_fusion.3) | copy-start | bytes 2359300
  463.2 5.0 %copy-start.24 = (f32[384,512]{1,0:T(8,128)S(1)}, f32[384,512]{1,0:T(8,128)}, u32[]{:S(2)}) copy-start(f32[384,512]{1,0:T(8,128)} %convolution_subtract_fusion) | copy-start | bytes 2359300
  463.3 5.0 %copy-start.25 = (f32[384,512]{1,0:T(8,128)S(1)}, f32[384,512]{1,0:T(8,128)}, u32[]{:S(2)}) copy-start(f32[384,512]{1,0:T(8,128)} %convolution_subtract_fusion.1) | copy-start | bytes 2359300
  464.9 3.4 copy-start.21
  464.9 3.4 copy-start.23
  (5 other events, 11.3 us)
Sparse Core Ops, SparseCore 0:
  10.8 72.5 all-gather.2
  103.3 147.5 all-reduce.2
  298.4 151.1 all-reduce.4
